TPU v7x, 256 devices: a whole 4x4x8 slice. The times are simulated.
256 devices in a mesh: tm: 32 (over y, x, core), space: 8 (over z).
Axes of the slice: x: 4, y: 4, z: 8, core: 2. Of those that a mesh axis runs over, the one named last changes fastest.
Arguments:
- latent_tokens: bfloat16 [64, 1792, 2240], P('tm', 'space'), may hold values from -6 to 6
- norm_gain: float32 [2240], replicated, may hold values from 0.5 to 1.5
- w_query: bfloat16 [2240, 1120], P('tm', 'space'), may hold values from -0.125 to 0.125
- w_key: bfloat16 [2240, 1120], P('tm', 'space'), may hold values from -0.125 to 0.125
- w_value: bfloat16 [2240, 1120], P('tm', 'space'), may hold values from -0.125 to 0.125
- out_gain: float32 [1120], replicated, may hold values from 0.5 to 1.5
- block_ids: int32 [64], P('tm'), may hold values from 0 to 15, never falling along the last dimension, each value on 1 to 8 neighbouring positions
Outputs:
- attended: bfloat16 [64, 1792, 1120], P('tm', 'space')
Inputs may be any that keep to these rules, and one draw needn't show every extreme that they name: `block_ids`: block numbers never fall from one frame to the next; each of the 16 blocks holds 1 to 8 frames and one holds exactly 8.
All inputs are finite; a program needn't handle non-finite values.
Results may differ from a plain program's by a relative error of at most 0.0065.
Values may be sent and summed in bfloat16 or wider, within the bound.
A program may use at most 192 MiB of HBM per device.

v0:
```python
import jax
import jax.numpy as jnp
from jax import lax
from jax.sharding import PartitionSpec as P

HEAD = 112
HEADS = 10


def prefix(value, axis, join, neutral):
    count, mine = (lax.axis_size(axis), lax.axis_index(axis))
    pieces = lax.all_gather(value, axis)
    so_far = jnp.full_like(value, 0) + jnp.asarray(neutral, value.dtype)

    def step(position, so_far):
        longer = join(so_far, pieces[position])
        return jnp.where(position < mine, longer, so_far)

    return lax.fori_loop(0, count - 1, step, so_far)


def carried_in(x, axis, join, neutral):
    count = lax.axis_size(axis)
    place = lax.axis_index(axis)
    ahead = count - 1 - place
    gathered = jax.tree.map(
        lambda a, kind: lax.all_gather(a.astype(kind), axis),
        x,
        jax.tree.map(lambda a: jnp.bfloat16 if a.dtype == jnp.float32 else a.dtype, x),
    )
    state = jax.tree.map(lambda a, e: jnp.zeros_like(a) + jnp.asarray(e, a.dtype), x, neutral)

    def one(step, state):
        source = count - 1 - step
        return join(
            state,
            jax.tree.map(
                lambda a, own: lax.dynamic_index_in_dim(a, source, 0, False).astype(own.dtype),
                gathered,
                x,
            ),
        )

    return lax.fori_loop(0, ahead, one, state)


def add_states(earlier, later):
    return earlier + later


def join_later(earlier, later):
    high_vacant, high_leading, high_uniform, high_running = earlier
    low_vacant, low_leading, low_uniform, low_running = later
    matching = (high_leading == low_leading).astype(jnp.float32)
    joined = low_uniform * matching * (1.0 - high_vacant)
    low_absent = low_vacant > 0.5
    leading = jnp.where(low_absent, high_leading, low_leading)
    vacant = low_vacant * high_vacant
    uniform = jnp.where(
        low_absent,
        high_uniform,
        low_uniform * (high_vacant + (1.0 - high_vacant) * high_uniform * matching),
    )
    running = jnp.where(low_absent, high_running, low_running + joined * high_running)
    return (vacant, leading, uniform, running)


def on_device(latent_tokens, norm_gain, w_query, w_key, w_value, out_gain, block_ids):
    frame_count, token_count, width = latent_tokens.shape
    row_count = frame_count * token_count
    values = latent_tokens.reshape(row_count, width).astype(jnp.float32)
    meansq = jnp.mean(values * values, axis=-1, keepdims=True)
    normed = (values * lax.rsqrt(meansq + 1e-06) * norm_gain).astype(jnp.bfloat16)
    stacked = jnp.stack((w_query, w_key, w_value))
    columns_full = lax.all_gather(stacked, "space", axis=2, tiled=True)
    projected = jnp.einsum(
        "rn,cnh->crh",
        normed,
        lax.all_gather(columns_full, "tm", axis=1, tiled=True),
        preferred_element_type=jnp.float32,
    )
    channels = projected.shape[2]
    query = jax.nn.relu(projected[0]).reshape(frame_count, token_count, HEADS, HEAD)
    key = (
        jax.nn.relu(projected[1])
        .astype(jnp.bfloat16)
        .reshape(frame_count, token_count, HEADS, HEAD)
    )
    value = projected[2].astype(jnp.bfloat16).reshape(frame_count, token_count, HEADS, HEAD)
    local_states = jnp.einsum("fthk,fthv->fhkv", key, value, preferred_element_type=jnp.float32)
    per_frame_state = lax.psum(local_states, "space")
    device_sum = jnp.sum(per_frame_state, axis=0)
    zero_state = jnp.zeros_like(device_sum)
    before = prefix(device_sum, "tm", add_states, zero_state)
    leading_id = block_ids[0]
    closing_id = block_ids[frame_count - 1]
    within_leading = (block_ids == leading_id).astype(jnp.float32)
    leading_sum = jnp.einsum(
        "o,owpe->wpe", within_leading, per_frame_state, precision=lax.Precision.HIGHEST
    )
    uniform_flag = jnp.min(within_leading)
    leading_float = leading_id.astype(jnp.float32)
    closing_float = closing_id.astype(jnp.float32)
    summary = (jnp.float32(0.0), leading_float, uniform_flag, leading_sum)
    identity = (jnp.float32(1.0), jnp.float32(0.0), jnp.float32(1.0), zero_state)
    vacant, leading, uniform, running = carried_in(summary, "tm", join_later, identity)
    reaches = (1.0 - vacant) * (leading == closing_float).astype(jnp.float32)
    trailing = reaches * running
    earlier_mask = (block_ids[None, :] <= block_ids[:, None]).astype(jnp.float32)
    in_closing = (block_ids == closing_id).astype(jnp.float32)
    carried = before[None] + jnp.einsum(
        "ij,jhkv->ihkv", earlier_mask, per_frame_state, precision=lax.Precision.HIGHEST
    )
    carried = carried + in_closing[:, None, None, None] * trailing[None]
    numerator = jnp.einsum("fthk,fhkv->fthv", query, carried, precision=lax.Precision.HIGHEST)
    head_meansq = jnp.mean(numerator * numerator, axis=-1, keepdims=True)
    result = numerator * lax.rsqrt(head_meansq + 1e-06) * out_gain.reshape(HEADS, HEAD)
    return result.reshape(frame_count, token_count, channels).astype(jnp.bfloat16)


def solution(mesh):
    placed = (
        P("tm", "space", None),
        P(),
        P("tm", "space"),
        P("tm", "space"),
        P("tm", "space"),
        P(),
        P("tm"),
    )
    return jax.shard_map(
        on_device, mesh=mesh, in_specs=placed, out_specs=P("tm", "space", None), check_vma=False
    )
```

profile of v0, /device:TPU:32, one launch (start us, length us, event | category | flops | bytes accessed | tf_op | source)
XLA Modules:
  0.0 544.3 jit_solution(14924308415363143273)
XLA Ops:
  7.7 29.9 %all_gather.33 = bf16[3,70,1120]{1,0,2:T(4,128)(2,1)S(1)} all-gather(bf16[3,70,140]{1,0,2:T(4,128)(2,1)S(1)} %copy.37), channel_id=1, replica_groups=mesh['tm'=32,'space'=8] {'space'}, dimensions={2}, use_global_device_ids=true | all-gather | bytes 529200 | tf_op jit(solution)/shard_map/all_gather | solution.py:75
  37.6 2.2 copy.38
  40.5 1.9 fusion.7
  42.4 84.1 %all-gather.6.cloned.1.call-done = bf16[3,2240,1120]{2,0,1:T(4,128)(2,1)} async-done(((bf16[3,70,1120]{2,0,1:T(4,128)(2,1)}), bf16[3,2240,1120]{2,0,1:T(4,128)(2,1)}) %all-gather.6.cloned.1.call-update) | async-done | bytes 15052816 | tf_op jit(solution)/shard_map/all_gather | solution.py:79
  126.5 14.1 %fusion.3 = f32[3,448,1120]{2,1,0:T(8,128)S(1)} fusion(bf16[3,2240,1120]{2,0,1:T(4,128)(2,1)} %all-gather.6.cloned.1.call-done, bf16[448,2240]{1,0:T(8,128)(2,1)} %fusion.7), kind=kOutput, calls=%fused_computation.5 | convolution fusion | flops 6743654400 | bytes 23080960 | tf_op jit(solution)/shard_map/rn,cnh->crh/dot_general | solution.py:76
  140.7 1.4 fusion.13
  142.1 1.5 copy-done.2
  143.6 3.4 reshape.84
  147.0 3.1 reshape.83
  150.1 3.1 fusion.16
  153.9 75.4 %all-reduce.6.cloned.1.call-done = f32[2,10,112,112]{3,2,1,0:T(8,128)} async-done(((f32[2,10,112,112]{3,2,1,0:T(8,128)}), f32[2,10,112,112]{3,2,1,0:T(8,128)}) %all-reduce.6.cloned.1.call-update) | async-done | bytes 1003536 | tf_op jit(solution)/shard_map/psum | solution.py:91
  229.3 4.7 fusion.20
  239.7 1.3 dynamic-update-slice.2
  241.0 63.4 %all-reduce.3 = (bf16[32]{0:T(256)(128)(2,1)S(1)}, bf16[32]{0:T(256)(128)(2,1)S(1)}, bf16[32]{0:T(256)(128)(2,1)S(1)}) all-reduce(bf16[32]{0:T(256)(128)(2,1)S(1)} %dynamic-update-slice, bf16[32]{0:T(256)(128)(2,1)S(1)} %dynamic-update-slice.1, bf16[32]{0:T(256)(128)(2,1)S(1)} %dynamic-update-slice.2), channel_id=1, replica_groups=mesh['tm'=32,'space'=8] {'tm'}, use_global_device_ids=true, to_apply=%add | all-reduce | flops 96 | bytes 384
  305.6 1.7 slice_maximum_fusion
  307.4 3.3 reshape.85
  310.7 177.9 %while.32 = (s32[]{:T(128)}, f32[]{:T(128)}, f32[]{:T(128)}, f32[10,112,112]{2,1,0:T(8,128)S(1)}, s32[]{:T(128)}, /*index=5*/bf16[32]{0:T(256)(128)(2,1)S(1)}, b...) while((s32[]{:T(128)}, f32[]{:T(128)}, f32[]{:T(128)}, ...), condition=%wide.region_7.8_spmd, body=%wide.region_6.7_spmd.sunk | while | flops 501773 | bytes 1254722 | solution.py:44
  320.9 1.3 fusion.33
  361.1 1.3 fusion.33
  488.6 38.9 %while.33 = (s32[]{:T(128)}, f32[10,112,112]{2,1,0:T(8,128)S(1)}, s32[]{:T(128)}, f32[32,10,112,112]{3,2,1,0:T(8,128)}, s32[]{:T(128)}, /*index=5*/s32[]{:T(128)}) while((s32[]{:T(128)}, f32[10,112,112]{2,1,0:T(8,128)S(1)}, s32[]{:T(128)}, f32[32,10,112,112]{3,2,1,0:T(8,128)}, s32[]{:T(128)}, /*index=5*/s32[]{:T(128)}) %tuple.73), condition=%wide.region_4.5_spmd.clone, body=%wide.region_3.4_spmd.clone.sunk | while | flops 376324 | bytes 1505381 | solution.py:19
  488.6 1.3 add_select_fusion.2
  527.6 3.3 fusion.15
  530.9 5.1 fusion.8
  536.4 1.4 copy.48
  (201 shorter events, 133.8 us)
Async XLA Ops:
  6.5 120.0 %all-gather.6.cloned.1.call-start = ((), (), s32[]{:S(2)}) async-start(), calls=%async_computation | async-start | bytes 21288960 | tf_op jit(solution)/shard_map/all_gather | solution.py:79
  6.5 33.4 %copy-start.1 = (bf16[2,224,2240]{2,1,0:T(8,128)(2,1)S(1)}, bf16[2,224,2240]{2,1,0:T(8,128)(2,1)}, u32[]{:S(2)}) copy-start(bf16[2,224,2240]{2,1,0:T(8,128)(2,1)} %param.11) | copy-start | bytes 6021124
  37.6 2.9 copy-start.5
  39.9 189.4 %all-reduce.6.cloned.1.call-start = ((), (), s32[]{:S(2)}) async-start(), calls=%async_computation.1 | async-start | bytes 2293760 | tf_op jit(solution)/shard_map/psum | solution.py:91
  140.7 2.9 copy-start.2
  150.1 3.2 copy-start.7
  153.3 157.4 %all-gather.10.cloned.1.call-start = ((), (), s32[]{:S(2)}) async-start(), calls=%async_computation.3 | async-start | bytes 9461760 | tf_op jit(solution)/shard_map/all_gather | solution.py:27
  229.3 5.6 %copy-start.3 = (f32[2,10,112,112]{3,2,1,0:T(8,128)S(1)}, f32[2,10,112,112]{3,2,1,0:T(8,128)}, u32[]{:S(2)}) copy-start(f32[2,10,112,112]{3,2,1,0:T(8,128)} %all-reduce.6.cloned.1.call-done) | copy-start | bytes 3010564
  234.0 2.5 copy-start.8
  234.0 71.0 %copy-start.6 = (f32[1120]{0:T(1024)S(1)}, f32[1120]{0:T(1024)}, u32[]{:S(2)}) copy-start(f32[1120]{0:T(1024)} %param.16) | copy-start | bytes 13444
  234.8 253.8 %all-gather.8.cloned.1.call-start = ((), (), s32[]{:S(2)}) async-start(), calls=%async_computation.2 | async-start | bytes 18923520 | tf_op jit(solution)/shard_map/all_gather | solution.py:12
  488.6 38.9 %copy-start.4 = (f32[2,10,112,112]{3,2,1,0:T(8,128)S(1)}, f32[2,10,112,112]{3,2,1,0:T(8,128)}, u32[]{:S(2)}) copy-start(f32[2,10,112,112]{3,2,1,0:T(8,128)} %all-reduce.6.cloned.1.call-done) | copy-start | bytes 3010564
  527.6 3.3 copy-start
Sparse Core Ops, SparseCore 0:
  40.0 86.5 all-gather.5
  153.4 75.8 all-reduce.5
  235.0 58.7 all-gather.9
  296.1 80.6 all-gather.7
where the time goes:
time: 548 us; the launch traced here: 544 us
  waiting for transfers between devices  160 us (29%)
  blocking collectives  93.3 us (17%)
  loops' own time  87.7 us (16%)
  other arithmetic  87.5 us (16%)
  local copies, waits for them, and re-layouts  71.2 us (13%)
  matrix products  30.4 us (6%)
  between operations  14.5 us (3%)
    another operation x1, loops' own time, carried_in(): return lax.fori_loop(0, ahead, one, state)  86.9 us
    all_gather x1, waiting for transfers between devices, on_device(): lax.all_gather(columns_full, 'tm', axis=1, tiled=True)  84.1 us
    psum x1, waiting for transfers between devices, on_device(): per_frame_state = lax.psum(local_states, 'space')  75.4 us
    unnamed x1, blocking collectives  63.4 us
    dynamic_slice x93, local copies, waits for them, and re-layouts, one(): lax.dynamic_index_in_dim(a, source, 0, False).astype(own.dtype)  52 us
    select_n x31, other arithmetic, join_later(): jnp.where(low_absent, high_running, low_running + joined * high_running)  38.9 us
    select_n x31, other arithmetic, step(): return jnp.where(position < mine, longer, so_far)  38.2 us
    all_gather x1, blocking collectives, on_device(): columns_full = lax.all_gather(stacked, 'space', axis=2, tiled=True)  29.9 us
  transfers between devices with their start and end apart: 4, of which 2 were waited for; matrix products, arithmetic and copies ran while one was open for 19% of the time, Pallas kernels for 0%

commit v1 on v0

--- a/solution.py
+++ b/solution.py
@@ -5,6 +5,12 @@
 
 HEAD = 112
 HEADS = 10
+
+
+def gather_by_exchange(x, axis, dim):
+    size = lax.axis_size(axis)
+    repeats = [size if d == dim else 1 for d in range(x.ndim)]
+    return lax.all_to_all(jnp.tile(x, repeats), axis, split_axis=dim, concat_axis=dim, tiled=True)
 
 
 def prefix(value, axis, join, neutral):
@@ -76,7 +82,7 @@
     projected = jnp.einsum(
         "rn,cnh->crh",
         normed,
-        lax.all_gather(columns_full, "tm", axis=1, tiled=True),
+        gather_by_exchange(columns_full, "tm", 1),
         preferred_element_type=jnp.float32,
     )
     channels = projected.shape[2]

time: 548 us -> 751 us (1.37)
  waiting for transfers between devices: 160 us -> 332 us
  loops' own time: 87.7 us -> 99.1 us
  local copies, waits for them, and re-layouts: 71.2 us -> 81.7 us
  starting transfers between devices: 0.13 us -> 7.87 us
    all_to_all x0 -> x1, waiting for transfers between devices: none -> 261 us  [gather_by_exchange(): lax.all_to_all(jnp.tile(x, repeats), axis, split_axis=dim, concat_axis=di...]
    all_gather x1 -> x0, waiting for transfers between devices: 84.1 us -> none  [on_device(): lax.all_gather(columns_full, 'tm', axis=1, tiled=True)]
    another operation x1, loops' own time: 86.9 us -> 98.3 us  [carried_in(): return lax.fori_loop(0, ahead, one, state)]
    all_to_all x0 -> x1, starting transfers between devices: none -> 7.56 us  [gather_by_exchange(): lax.all_to_all(jnp.tile(x, repeats), axis, split_axis=dim, concat_axis=di...]
  transfers between devices with their start and end apart: 4 -> 4, of which waited for: 2 -> 2; matrix products, arithmetic and copies ran while one was open for 19% -> 15% of each run, Pallas kernels for 0% -> 0%
where the time goes in v1:
time: 751 us; the launch traced here: 746 us
  waiting for transfers between devices  332 us (44%)
  loops' own time  99.1 us (13%)
  blocking collectives  93.3 us (12%)
  other arithmetic  87.7 us (12%)
  local copies, waits for them, and re-layouts  81.7 us (11%)
  matrix products  30.3 us (4%)
  between operations  14.7 us (2%)
  starting transfers between devices  7.87 us (1%)
    all_to_all x1, waiting for transfers between devices, gather_by_exchange(): lax.all_to_all(jnp.tile(x, repeats), axis, split_axis=dim, concat_axis=di...  261 us
    another operation x1, loops' own time, carried_in(): return lax.fori_loop(0, ahead, one, state)  98.3 us
    psum x1, waiting for transfers between devices, on_device(): per_frame_state = lax.psum(local_states, 'space')  70.7 us
    unnamed x1, blocking collectives  63.4 us
    dynamic_slice x93, local copies, waits for them, and re-layouts, one(): lax.dynamic_index_in_dim(a, source, 0, False).astype(own.dtype)  55.8 us
    select_n x31, other arithmetic, join_later(): jnp.where(low_absent, high_running, low_running + joined * high_running)  39.1 us
    select_n x31, other arithmetic, step(): return jnp.where(position < mine, longer, so_far)  38.2 us
    all_gather x1, blocking collectives, on_device(): columns_full = lax.all_gather(stacked, 'space', axis=2, tiled=True)  29.9 us
  transfers between devices with their start and end apart: 4, of which 2 were waited for; matrix products, arithmetic and copies ran while one was open for 15% of the time, Pallas kernels for 0%

profile of v1, /device:TPU:32, one launch (start us, length us, event | category | flops | bytes accessed | tf_op | source)
XLA Modules:
  0.0 746.4 jit_solution(4015341823566589168)
XLA Ops:
  7.6 29.9 %all_gather.30 = bf16[3,70,1120]{1,0,2:T(4,128)(2,1)S(1)} all-gather(bf16[3,70,140]{1,0,2:T(4,128)(2,1)S(1)} %copy.38), channel_id=1, replica_groups=mesh['tm'=32,'space'=8] {'space'}, dimensions={2}, use_global_device_ids=true | all-gather | bytes 529200 | tf_op jit(solution)/shard_map/all_gather | solution.py:81
  37.4 1.5 copy.61
  39.0 7.3 tile.4.clone
  46.2 7.6 %all-to-all-start = ((bf16[3,2240,1120]{2,0,1:T(4,128)(2,1)}), bf16[3,2240,1120]{2,0,1:T(4,128)(2,1)}, u32[]{:S(2)}, u32[]{:S(2)}) async-start(bf16[3,2240,1120]{2,0,1:T(4,128)(2,1)} %bitcast.65), calls=%async_computation | async-start | bytes 41287680 | tf_op jit(solution)/shard_map/all_to_all | solution.py:13
  54.5 1.9 fusion.7
  56.4 261.0 %all-to-all-done = bf16[3,2240,1120]{2,0,1:T(4,128)(2,1)} async-done(((bf16[3,2240,1120]{2,0,1:T(4,128)(2,1)}), bf16[3,2240,1120]{2,0,1:T(4,128)(2,1)}, u32[]{:S(2)}, u32[]{:S(2)}) %all-to-all-start) | async-done | bytes 15052832 | tf_op jit(solution)/shard_map/all_to_all | solution.py:13
  317.3 14.1 %fusion.3 = f32[3,448,1120]{2,1,0:T(8,128)S(1)} fusion(bf16[3,2240,1120]{2,0,1:T(4,128)(2,1)} %all-to-all-done, bf16[448,2240]{1,0:T(8,128)(2,1)} %fusion.7), kind=kOutput, calls=%fused_computation.5 | convolution fusion | flops 6743654400 | bytes 23080960 | tf_op jit(solution)/shard_map/rn,cnh->crh/dot_general | solution.py:82
  331.4 1.4 fusion.13
  332.8 1.5 copy-done.2
  334.3 3.4 reshape.88
  337.8 3.1 reshape.87
  340.9 3.1 fusion.16
  344.7 70.7 %all-reduce.6.cloned.1.call-done = f32[2,10,112,112]{3,2,1,0:T(8,128)} async-done(((f32[2,10,112,112]{3,2,1,0:T(8,128)}), f32[2,10,112,112]{3,2,1,0:T(8,128)}) %all-reduce.6.cloned.1.call-update) | async-done | bytes 1003536 | tf_op jit(solution)/shard_map/psum | solution.py:97
  415.4 4.8 fusion.20
  427.6 63.4 %all-reduce.3 = (bf16[32]{0:T(256)(128)(2,1)S(1)}, bf16[32]{0:T(256)(128)(2,1)S(1)}, bf16[32]{0:T(256)(128)(2,1)S(1)}) all-reduce(bf16[32]{0:T(256)(128)(2,1)S(1)} %dynamic-update-slice, bf16[32]{0:T(256)(128)(2,1)S(1)} %dynamic-update-slice.1, bf16[32]{0:T(256)(128)(2,1)S(1)} %dynamic-update-slice.2), channel_id=1, replica_groups=mesh['tm'=32,'space'=8] {'tm'}, use_global_device_ids=true, to_apply=%add | all-reduce | flops 96 | bytes 384
  492.4 1.8 slice_maximum_fusion
  494.1 3.3 reshape.89
  497.5 193.3 %while.32 = (s32[]{:T(128)}, f32[]{:T(128)}, f32[]{:T(128)}, f32[10,112,112]{2,1,0:T(8,128)S(1)}, s32[]{:T(128)}, /*index=5*/bf16[32]{0:T(256)(128)(2,1)S(1)}, b...) while((s32[]{:T(128)}, f32[]{:T(128)}, f32[]{:T(128)}, ...), condition=%wide.region_7.8_spmd, body=%wide.region_6.7_spmd.sunk | while | flops 501773 | bytes 1254722 | solution.py:50
  521.1 1.3 fusion.33
  558.6 1.3 fusion.33
  690.8 38.9 %while.33 = (s32[]{:T(128)}, f32[10,112,112]{2,1,0:T(8,128)S(1)}, s32[]{:T(128)}, f32[32,10,112,112]{3,2,1,0:T(8,128)}, s32[]{:T(128)}, /*index=5*/s32[]{:T(128)}) while((s32[]{:T(128)}, f32[10,112,112]{2,1,0:T(8,128)S(1)}, s32[]{:T(128)}, f32[32,10,112,112]{3,2,1,0:T(8,128)}, s32[]{:T(128)}, /*index=5*/s32[]{:T(128)}) %tuple.71), condition=%wide.region_4.5_spmd.clone, body=%wide.region_3.4_spmd.clone.sunk | while | flops 376324 | bytes 1505381 | solution.py:25
  729.8 3.3 fusion.15
  733.1 5.1 fusion.8
  738.5 1.4 copy.50
  (201 shorter events, 140.7 us)
Async XLA Ops:
  46.2 7.6 %copy-start.1 = (bf16[2,224,2240]{2,1,0:T(8,128)(2,1)S(1)}, bf16[2,224,2240]{2,1,0:T(8,128)(2,1)}, u32[]{:S(2)}) copy-start(bf16[2,224,2240]{2,1,0:T(8,128)(2,1)} %param.11) | copy-start | bytes 6021124
  46.2 271.1 %all-to-all-start = ((bf16[3,2240,1120]{2,0,1:T(4,128)(2,1)}), bf16[3,2240,1120]{2,0,1:T(4,128)(2,1)}, u32[]{:S(2)}, u32[]{:S(2)}) async-start(bf16[3,2240,1120]{2,0,1:T(4,128)(2,1)} %bitcast.65), calls=%async_computation | async-start | bytes 41287680 | tf_op jit(solution)/shard_map/all_to_all | solution.py:13
  53.8 0.7 copy-start.5
  53.8 361.6 %all-reduce.6.cloned.1.call-start = ((), (), s32[]{:S(2)}) async-start(), calls=%async_computation.1 | async-start | bytes 2293760 | tf_op jit(solution)/shard_map/psum | solution.py:97
  331.4 2.9 copy-start.2
  340.9 3.2 copy-start.7
  344.0 153.4 %all-gather.7.cloned.1.call-start = ((), (), s32[]{:S(2)}) async-start(), calls=%async_computation.3 | async-start | bytes 9461760 | tf_op jit(solution)/shard_map/all_gather | solution.py:33
  415.4 5.8 copy-start.3
  420.2 2.7 copy-start.8
  420.2 71.5 %copy-start.6 = (f32[1120]{0:T(1024)S(1)}, f32[1120]{0:T(1024)}, u32[]{:S(2)}) copy-start(f32[1120]{0:T(1024)} %param.16) | copy-start | bytes 13444
  421.0 269.8 %all-gather.5.cloned.1.call-start = ((), (), s32[]{:S(2)}) async-start(), calls=%async_computation.2 | async-start | bytes 18923520 | tf_op jit(solution)/shard_map/all_gather | solution.py:18
  690.8 38.9 %copy-start.4 = (f32[2,10,112,112]{3,2,1,0:T(8,128)S(1)}, f32[2,10,112,112]{3,2,1,0:T(8,128)}, u32[]{:S(2)}) copy-start(f32[2,10,112,112]{3,2,1,0:T(8,128)} %all-reduce.6.cloned.1.call-done) | copy-start | bytes 3010564
  729.8 3.3 copy-start
Sparse Core Ops, SparseCore 0:
  344.1 71.1 all-reduce.5
  421.1 58.7 all-gather.6
  482.5 80.7 all-gather.4
